TPU v7x, 32 devices: a whole 2x2x4 slice. The times are simulated.
32 devices in a mesh: groups: 2 (over y), ctx: 4 (over z), wt: 2 (over x), sub: 2 (over core).
Axes of the slice: x: 2, y: 2, z: 4, core: 2. Of those that a mesh axis runs over, the one named last changes fastest.
Arguments:
- queries: bfloat16 [16, 32, 128, 576], P(('groups', 'ctx'), None, ('wt', 'sub')), parts along dimension 0, may hold values from -80 to 80
- selection: int32 [16, 4, 2], P(('groups', 'ctx')), parts along dimension 0, may hold values from -1 to 15, as said below
- latent_cache: bfloat16 [128, 64, 576], P(('groups', 'ctx')), parts along dimension 0, may hold values from -8 to 8
- value_up: bfloat16 [128, 512, 128], P(None, ('wt', 'sub')), may hold values from -1 to 1
Outputs:
- attended: bfloat16 [16, 32, 128, 128], P(('groups', 'ctx'), None, ('wt', 'sub')), parts along dimension 0
There are 2 independent parts, one for each index of `groups`. A program takes and returns all parts, laid end to end along the dimension named above; an argument that names none is the same for every part. Nothing has to cross between parts.
Inputs may be any that keep to these rules, and one draw needn't show every extreme that they name: `selection`: entry [c, o, s] is the number of a block among the 16 of owner o, or -1 for an empty slot; in an owner's slots live entries come first and differ. Each query block has 4 live entries in all, and in every query block some owner fills all 2 slots.
All inputs are finite; a program needn't handle non-finite values.
Results may differ from a plain program's by a relative error of at most 0.008.
Values may be sent and summed in bfloat16 or wider, within the bound.
No kernel may reach another device: no remote copies, remote signals or barrier semaphores. Data moves between devices by JAX's collectives and lax.ppermute only.
A program may use at most 128 MiB of HBM per device.

v0:
```python
import jax
import jax.numpy as jnp
from jax import lax
from jax.sharding import PartitionSpec as P

LAT = 512
ROPE = 64
NOPE = 128


def attend(query, blocks, chosen):
    width = query.shape[2]
    owners = chosen.shape[0]
    count = chosen.shape[0] * chosen.shape[1]
    live = (chosen >= 0).reshape(-1)
    ranked = jnp.where(live, 0, count).astype(jnp.int32) + jnp.arange(count, dtype=jnp.int32)
    picked = jnp.argsort(ranked)[:owners]
    keys = blocks.reshape(count, blocks.shape[2], width)[picked].reshape(-1, width)
    rows = query.reshape(-1, width)
    scores = jnp.einsum("rd,kd->rk", rows, keys, preferred_element_type=jnp.float32)
    scores = scores * jnp.float32((NOPE + ROPE) ** (-0.5))
    expo = jnp.exp(scores - jnp.max(scores, axis=1, keepdims=True))
    totals = jnp.sum(expo, axis=1, keepdims=True)
    weights = expo.astype(jnp.bfloat16)
    latent = (jnp.dot(weights, keys[:, :LAT], preferred_element_type=jnp.float32) / totals).astype(
        jnp.bfloat16
    )
    return latent.reshape(query.shape[0], query.shape[1], LAT)


def per_device(queries, selection, latent_cache, value_up):
    owners = lax.axis_size("ctx")
    spans, per_span, heads_here, width = queries.shape
    slots = selection.shape[2]
    block_len = latent_cache.shape[1]

    def serve(asked):
        safe = jnp.clip(asked, 0, latent_cache.shape[0] - 1)
        return lax.all_to_all(latent_cache[safe], "ctx", split_axis=0, concat_axis=0, tiled=True)

    def fetch(wanted):
        half = slots // 2
        mine = lax.dynamic_slice_in_dim(wanted, lax.axis_index("sub") * half, half, 2)
        count = mine.shape[1] * mine.shape[2]
        fetched = serve(
            lax.all_to_all(
                mine.reshape(owners, count), "ctx", split_axis=0, concat_axis=0, tiled=True
            )
        )
        fetched = fetched.reshape(owners, mine.shape[1], mine.shape[2], block_len, width)
        fetched = lax.all_gather(fetched, "sub", axis=2, tiled=True)
        return fetched

    wanted_all = jnp.transpose(selection, (1, 0, 2))
    gathered = [fetch(wanted_all[:, index : index + 1])[:, 0] for index in range(spans)]
    latents = [attend(queries[index], gathered[index], selection[index]) for index in range(spans)]
    flat = jnp.stack(latents).reshape(spans * per_span, heads_here, LAT)
    my_weights = lax.all_to_all(value_up, ("wt", "sub"), split_axis=0, concat_axis=1, tiled=True)
    summed = jnp.einsum("nhl,hlv->nhv", flat, my_weights, preferred_element_type=jnp.float32)
    return summed.astype(jnp.bfloat16).reshape(spans, per_span, heads_here, my_weights.shape[2])


def solution(mesh):
    placed = (
        P(("groups", "ctx"), None, ("wt", "sub"), None),
        P(("groups", "ctx"), None, None),
        P(("groups", "ctx"), None, None),
        P(None, ("wt", "sub"), None),
    )
    return jax.shard_map(
        per_device,
        mesh=mesh,
        in_specs=placed,
        out_specs=P(("groups", "ctx"), None, ("wt", "sub"), None),
        check_vma=False,
    )
```

profile of v0, /device:TPU:0, one launch (start us, length us, event | category | flops | bytes accessed | tf_op | source)
XLA Modules:
  0.0 102.0 jit_solution(10457877809274622)
XLA Ops:
  0.0 0.9 copy.21
  0.9 0.7 constant_dynamic-slice_fusion.1
  1.6 6.3 %all-to-all-start = ((s32[4,1,1]{2,1,0:T(1,128)}), s32[4,1,1]{2,1,0:T(1,128)S(1)}, u32[]{:S(2)}, u32[]{:S(2)}) async-start(s32[4,1,1]{2,1,0:T(1,128)} %constant_dynamic-slice_fusion.1), calls=%async_computation | async-start | bytes 4096 | tf_op jit(solution)/shard_map/all_to_all | solution.py:46
  7.9 0.7 constant_dynamic-slice_fusion
  8.6 4.8 %all-to-all-done = s32[4,1,1]{2,1,0:T(1,128)S(1)} async-done(((s32[4,1,1]{2,1,0:T(1,128)}), s32[4,1,1]{2,1,0:T(1,128)S(1)}, u32[]{:S(2)}, u32[]{:S(2)}) %all-to-all-start) | async-done | bytes 48 | tf_op jit(solution)/shard_map/all_to_all | solution.py:46
  13.3 3.2 %all-to-all-start.2 = ((s32[4,1,1]{2,1,0:T(1,128)}), s32[4,1,1]{2,1,0:T(1,128)S(1)}, u32[]{:S(2)}, u32[]{:S(2)}) async-start(s32[4,1,1]{2,1,0:T(1,128)} %constant_dynamic-slice_fusion), calls=%async_computation.2 | async-start | bytes 4096 | tf_op jit(solution)/shard_map/all_to_all | solution.py:46
  16.7 1.3 %gather_fusion = bf16[4,64,576]{2,1,0:T(8,128)(2,1)} fusion(bf16[16,64,576]{2,1,0:T(8,128)(2,1)S(1)} %copy-done, s32[1024]{0:T(1024)S(1)} %pad_clamp_fusion.3), kind=kCustom, calls=%fused_computation | custom fusion | bytes 589840 | tf_op jit(solution)/shard_map/gather | solution.py:39
  18.0 4.0 %all-to-all-done.2 = s32[4,1,1]{2,1,0:T(1,128)S(1)} async-done(((s32[4,1,1]{2,1,0:T(1,128)}), s32[4,1,1]{2,1,0:T(1,128)S(1)}, u32[]{:S(2)}, u32[]{:S(2)}) %all-to-all-start.2) | async-done | bytes 48 | tf_op jit(solution)/shard_map/all_to_all | solution.py:46
  22.0 3.5 %all-to-all-start.1 = ((bf16[4,1,64,576]{3,2,1,0:T(8,128)(2,1)}), bf16[4,1,64,576]{3,2,1,0:T(8,128)(2,1)S(1)}, u32[]{:S(2)}, u32[]{:S(2)}) async-start(bf16[4,1,64,576]{3,2,1,0:T(8,128)(2,1)} %bitcast.1), calls=%async_computation.1 | async-start | bytes 655360 | tf_op jit(solution)/shard_map/all_to_all | solution.py:39
  25.7 1.3 %gather_fusion.2 = bf16[4,64,576]{2,1,0:T(8,128)(2,1)} fusion(bf16[16,64,576]{2,1,0:T(8,128)(2,1)S(1)} %copy-done, s32[1024]{0:T(1024)S(1)} %pad_clamp_fusion.1), kind=kCustom, calls=%fused_computation.2 | custom fusion | bytes 589840 | tf_op jit(solution)/shard_map/gather | solution.py:39
  27.0 5.8 %all-to-all-done.1 = bf16[4,1,64,576]{3,2,1,0:T(8,128)(2,1)S(1)} async-done(((bf16[4,1,64,576]{3,2,1,0:T(8,128)(2,1)}), bf16[4,1,64,576]{3,2,1,0:T(8,128)(2,1)S(1)}, u32[]{:S(2)}, u32[]{:S(2)}) %all-to-all-start.1) | async-done | bytes 294944 | tf_op jit(solution)/shard_map/all_to_all | solution.py:39
  32.8 3.6 %all-to-all-start.3 = ((bf16[4,1,64,576]{3,2,1,0:T(8,128)(2,1)}), bf16[4,1,64,576]{3,2,1,0:T(8,128)(2,1)S(1)}, u32[]{:S(2)}, u32[]{:S(2)}) async-start(bf16[4,1,64,576]{3,2,1,0:T(8,128)(2,1)} %bitcast.6), calls=%async_computation.3 | async-start | bytes 655360 | tf_op jit(solution)/shard_map/all_to_all | solution.py:39
  36.7 6.9 %all-to-all-done.3 = bf16[4,1,64,576]{3,2,1,0:T(8,128)(2,1)S(1)} async-done(((bf16[4,1,64,576]{3,2,1,0:T(8,128)(2,1)}), bf16[4,1,64,576]{3,2,1,0:T(8,128)(2,1)S(1)}, u32[]{:S(2)}, u32[]{:S(2)}) %all-to-all-start.3) | async-done | bytes 294944 | tf_op jit(solution)/shard_map/all_to_all | solution.py:39
  43.7 0.7 copy-done.2
  44.4 4.9 %all-to-all-start.4 = ((bf16[128,128,128]{2,1,0:T(8,128)(2,1)}), bf16[128,128,128]{2,1,0:T(8,128)(2,1)}, u32[]{:S(2)}, u32[]{:S(2)}) async-start(bf16[128,128,128]{2,1,0:T(8,128)(2,1)} %param.7), calls=%async_computation.4 | async-start | bytes 8388608 | tf_op jit(solution)/shard_map/all_to_all | solution.py:58
  49.3 1.0 sort.31
  50.2 1.0 sort.32
  51.3 3.1 %fusion.12 = (bf16[1,32,32,576]{3,2,1,0:T(8,128)(2,1)S(1)}, bf16[1,32,32,576]{3,2,1,0:T(8,128)(2,1)}) fusion(bf16[2,32,32,576]{3,2,1,0:T(8,128)(2,1)} %param.4), kind=kLoop, calls=%fused_computation.36 | loop fusion | bytes 4718592 | tf_op jit(solution)/shard_map/slice | solution.py:56
  54.4 2.3 %all-gather.1 = bf16[4,2,64,576]{3,2,1,0:T(8,128)(2,1)S(1)} all-gather(bf16[4,1,64,576]{3,2,1,0:T(8,128)(2,1)S(1)} %copy-done.3), channel_id=3, replica_groups=mesh['groups'=2,'ctx'=4,'wt'=2,'sub'=2] {'sub'}, dimensions={1}, use_global_device_ids=true | all-gather | bytes 884736 | tf_op jit(solution)/shard_map/all_gather | solution.py:51
  56.7 1.3 %gather_fusion.3 = bf16[4,64,576]{2,1,0:T(8,128)(2,1)} fusion(bf16[8,64,576]{2,1,0:T(8,128)(2,1)S(1)} %bitcast.30, s32[1024]{0:T(1024)S(1)} %pad_clamp_fusion), kind=kCustom, calls=%fused_computation.3 | custom fusion | bytes 589840 | tf_op jit(solution)/shard_map/gather | solution.py:18
  58.0 2.5 %all-gather = bf16[4,2,64,576]{3,2,1,0:T(8,128)(2,1)S(1)} all-gather(bf16[4,1,64,576]{3,2,1,0:T(8,128)(2,1)} %copy-done.1), channel_id=2, replica_groups=mesh['groups'=2,'ctx'=4,'wt'=2,'sub'=2] {'sub'}, dimensions={1}, use_global_device_ids=true | all-gather | bytes 884736 | tf_op jit(solution)/shard_map/all_gather | solution.py:51
  60.5 1.3 %gather_fusion.1 = bf16[4,64,576]{2,1,0:T(8,128)(2,1)} fusion(bf16[8,64,576]{2,1,0:T(8,128)(2,1)S(1)} %bitcast.31, s32[1024]{0:T(1024)S(1)} %pad_clamp_fusion.2), kind=kCustom, calls=%fused_computation.1 | custom fusion | bytes 589840 | tf_op jit(solution)/shard_map/gather | solution.py:18
  61.8 2.1 %fusion.14 = (f32[1024]{0:T(1024)S(1)}, f32[256,1024]{1,0:T(8,128)S(1)}) fusion(bf16[256,576]{1,0:T(8,128)(2,1)} %bitcast.32, bf16[1024,576]{1,0:T(8,128)(2,1)} %bitcast.28), kind=kOutput, calls=%fused_computation.38 | convolution fusion | flops 302513152 | bytes 2527232 | tf_op jit(solution)/shard_map/rd,kd->rk/dot_general | solution.py:20
  64.1 0.6 fusion.15
  65.0 0.5 divide_convert_fusion
  65.5 0.5 divide_convert_fusion.1
  66.1 0.2 pad_maximum_fusion
  66.3 1.2 %copy.24 = bf16[2,32,32,512]{3,1,0,2:T(8,128)(2,1)S(1)} copy(bf16[2,32,32,512]{3,2,1,0:T(8,128)(2,1)S(1)} %pad_maximum_fusion) | data formatting | bytes 4194304 | tf_op jit(solution)/shard_map/stack | solution.py:57
  67.4 30.0 %all-to-all-done.4 = bf16[128,128,128]{2,1,0:T(8,128)(2,1)} async-done(((bf16[128,128,128]{2,1,0:T(8,128)(2,1)}), bf16[128,128,128]{2,1,0:T(8,128)(2,1)}, u32[]{:S(2)}, u32[]{:S(2)}) %all-to-all-start.4) | async-done | bytes 4194336 | tf_op jit(solution)/shard_map/all_to_all | solution.py:58
  97.5 2.5 %copy.25 = bf16[4,32,128,128]{3,2,0,1:T(8,128)(2,1)S(1)} copy(bf16[4,32,128,128]{3,2,1,0:T(8,128)(2,1)} %bitcast.12) | data formatting | bytes 8388608 | tf_op jit(solution)/shard_map/all_to_all | solution.py:58
  100.0 0.9 convolution_convert_fusion
  100.8 1.1 %copy.26 = bf16[2,32,32,128]{3,2,1,0:T(8,128)(2,1)} copy(bf16[2,32,32,128]{3,1,0,2:T(8,128)(2,1)S(1)} %bitcast.29) | data formatting | bytes 1048576 | tf_op jit(solution)/shard_map/reshape | solution.py:60
  (33 shorter events, 1.3 us)
Async XLA Ops:
  0.0 16.7 %copy-start = (bf16[16,64,576]{2,1,0:T(8,128)(2,1)S(1)}, bf16[16,64,576]{2,1,0:T(8,128)(2,1)}, u32[]{:S(2)}) copy-start(bf16[16,64,576]{2,1,0:T(8,128)(2,1)} %param.6) | copy-start | bytes 3538948
  0.0 36.4 %copy-start.6 = (s32[2,4,2]{1,2,0:T(2,128)S(1)}, s32[2,4,2]{1,2,0:T(2,128)}, u32[]{:S(2)}) copy-start(s32[2,4,2]{1,2,0:T(2,128)} %param.5) | copy-start | bytes 196
  1.6 11.8 %all-to-all-start = ((s32[4,1,1]{2,1,0:T(1,128)}), s32[4,1,1]{2,1,0:T(1,128)S(1)}, u32[]{:S(2)}, u32[]{:S(2)}) async-start(s32[4,1,1]{2,1,0:T(1,128)} %constant_dynamic-slice_fusion.1), calls=%async_computation | async-start | bytes 4096 | tf_op jit(solution)/shard_map/all_to_all | solution.py:46
  13.3 8.7 %all-to-all-start.2 = ((s32[4,1,1]{2,1,0:T(1,128)}), s32[4,1,1]{2,1,0:T(1,128)S(1)}, u32[]{:S(2)}, u32[]{:S(2)}) async-start(s32[4,1,1]{2,1,0:T(1,128)} %constant_dynamic-slice_fusion), calls=%async_computation.2 | async-start | bytes 4096 | tf_op jit(solution)/shard_map/all_to_all | solution.py:46
  22.0 10.7 %all-to-all-start.1 = ((bf16[4,1,64,576]{3,2,1,0:T(8,128)(2,1)}), bf16[4,1,64,576]{3,2,1,0:T(8,128)(2,1)S(1)}, u32[]{:S(2)}, u32[]{:S(2)}) async-start(bf16[4,1,64,576]{3,2,1,0:T(8,128)(2,1)} %bitcast.1), calls=%async_computation.1 | async-start | bytes 655360 | tf_op jit(solution)/shard_map/all_to_all | solution.py:39
  32.8 10.9 %copy-start.1 = (bf16[4,1,64,576]{3,2,1,0:T(8,128)(2,1)}, bf16[4,1,64,576]{3,2,1,0:T(8,128)(2,1)S(1)}, u32[]{:S(2)}) copy-start(bf16[4,1,64,576]{3,2,1,0:T(8,128)(2,1)S(1)} %all-to-all-done.1) | copy-start | bytes 884740
  32.8 10.9 %all-to-all-start.3 = ((bf16[4,1,64,576]{3,2,1,0:T(8,128)(2,1)}), bf16[4,1,64,576]{3,2,1,0:T(8,128)(2,1)S(1)}, u32[]{:S(2)}, u32[]{:S(2)}) async-start(bf16[4,1,64,576]{3,2,1,0:T(8,128)(2,1)} %bitcast.6), calls=%async_computation.3 | async-start | bytes 655360 | tf_op jit(solution)/shard_map/all_to_all | solution.py:39
  43.7 0.7 copy-start.2
  44.4 53.1 %all-to-all-start.4 = ((bf16[128,128,128]{2,1,0:T(8,128)(2,1)}), bf16[128,128,128]{2,1,0:T(8,128)(2,1)}, u32[]{:S(2)}, u32[]{:S(2)}) async-start(bf16[128,128,128]{2,1,0:T(8,128)(2,1)} %param.7), calls=%async_computation.4 | async-start | bytes 8388608 | tf_op jit(solution)/shard_map/all_to_all | solution.py:58
  51.3 3.1 %copy-start.3 = (bf16[4,1,64,576]{3,2,1,0:T(8,128)(2,1)S(1)}, bf16[4,1,64,576]{3,2,1,0:T(8,128)(2,1)}, u32[]{:S(2)}) copy-start(bf16[4,1,64,576]{3,2,1,0:T(8,128)(2,1)} %copy-done.2) | copy-start | bytes 884740
  61.8 2.3 %copy-start.5 = (bf16[4,64,576]{2,1,0:T(8,128)(2,1)S(1)}, bf16[4,64,576]{2,1,0:T(8,128)(2,1)}, u32[]{:S(2)}) copy-start(bf16[4,64,576]{2,1,0:T(8,128)(2,1)} %gather_fusion.1) | copy-start | bytes 884740
  64.1 1.0 copy-start.4
where the time goes:
time: 103 us; the launch traced here: 102 us
  waiting for transfers between devices  51.5 us (50%)
  starting transfers between devices  21.5 us (21%)
  local copies, waits for them, and re-layouts  16.6 us (16%)
  blocking collectives  4.81 us (5%)
  matrix products  4.57 us (4%)
  other arithmetic  2.85 us (3%)
    all_to_all x1, waiting for transfers between devices, per_device(): lax.all_to_all(value_up, ('wt', 'sub'), split_axis=0, concat_axis=1, tile...  30 us
    all_to_all x2, waiting for transfers between devices, serve(): lax.all_to_all(latent_cache[safe], 'ctx', split_axis=0, concat_axis=0, ti...  12.7 us
    all_to_all x2, starting transfers between devices, fetch(): lax.all_to_all(mine.reshape(owners, count), 'ctx', split_axis=0, concat_a...  9.57 us
    all_to_all x2, waiting for transfers between devices, fetch(): lax.all_to_all(mine.reshape(owners, count), 'ctx', split_axis=0, concat_a...  8.76 us
    all_to_all x2, starting transfers between devices, serve(): lax.all_to_all(latent_cache[safe], 'ctx', split_axis=0, concat_axis=0, ti...  7.06 us
    all_to_all x1, starting transfers between devices, per_device(): lax.all_to_all(value_up, ('wt', 'sub'), split_axis=0, concat_axis=1, tile...  4.86 us
    all_gather x2, blocking collectives, fetch(): fetched = lax.all_gather(fetched, 'sub', axis=2, tiled=True)  4.81 us
    slice x1, local copies, waits for them, and re-layouts, per_device(): queries[index]  3.08 us
  transfers between devices with their start and end apart: 5, of which 5 were waited for; matrix products, arithmetic and copies ran while one was open for 17% of the time, Pallas kernels for 0%

commit v1 on v0

--- a/solution.py
+++ b/solution.py
@@ -2,6 +2,7 @@
 import jax.numpy as jnp
 from jax import lax
 from jax.sharding import PartitionSpec as P
+from jax.lax import axis_index, axis_size, ppermute
 
 LAT = 512
 ROPE = 64
@@ -42,11 +43,29 @@
         half = slots // 2
         mine = lax.dynamic_slice_in_dim(wanted, lax.axis_index("sub") * half, half, 2)
         count = mine.shape[1] * mine.shape[2]
-        fetched = serve(
-            lax.all_to_all(
-                mine.reshape(owners, count), "ctx", split_axis=0, concat_axis=0, tiled=True
-            )
-        )
+
+        def manage_the_steps_all(vals):
+            mesh_ax = "ctx"
+            e_now = axis_size(mesh_ax)
+            carry, later = (e_now, axis_index(mesh_ax))
+            top = vals.shape[0] // carry
+            v_next = list(vals.shape)
+            v_next[0] = top
+            left_arr = v_next[0]
+            v_next[0] = left_arr * carry
+            everything = jnp.zeros(v_next, vals.dtype)
+            for tick in range(carry):
+                all_values = lax.dynamic_slice_in_dim(vals, (later ^ tick) * top, top, axis=0)
+                if tick:
+                    all_values = ppermute(
+                        all_values, mesh_ax, [(dev_i, dev_i ^ tick) for dev_i in range(carry)]
+                    )
+                everything = lax.dynamic_update_slice_in_dim(
+                    everything, all_values, (later ^ tick) * left_arr, axis=0
+                )
+            return everything
+
+        fetched = serve(manage_the_steps_all(mine.reshape(owners, count)))
         fetched = fetched.reshape(owners, mine.shape[1], mine.shape[2], block_len, width)
         fetched = lax.all_gather(fetched, "sub", axis=2, tiled=True)
         return fetched

time: 103 us -> 103 us (level)
  waiting for transfers between devices: 51.5 us -> 45 us
  local copies, waits for them, and re-layouts: 16.6 us -> 22.2 us
  starting transfers between devices: 21.5 us -> 22.8 us
    ppermute x0 -> x6, starting transfers between devices: none -> 10.2 us  [manage_the_steps_all(): ppermute(all_values, mesh_ax, [(dev_i, dev_i ^ tick) for dev_i in range(c...]
    all_to_all x2 -> x0, starting transfers between devices: 9.57 us -> none  [fetch(): lax.all_to_all(mine.reshape(owners, count), 'ctx', split_axis=0, concat_a...]
    all_to_all x2 -> x0, waiting for transfers between devices: 8.76 us -> none  [fetch(): lax.all_to_all(mine.reshape(owners, count), 'ctx', split_axis=0, concat_a...]
    dynamic_update_slice x0 -> x8, local copies, waits for them, and re-layouts: none -> 5.69 us  [manage_the_steps_all(): lax.dynamic_update_slice_in_dim(everything, all_values, (later ^ tick) *...]
    all_to_all x2, waiting for transfers between devices: 12.7 us -> 14 us  [serve(): lax.all_to_all(latent_cache[safe], 'ctx', split_axis=0, concat_axis=0, ti...]
  transfers between devices with their start and end apart: 5 -> 9, of which waited for: 5 -> 4; matrix products, arithmetic and copies ran while one was open for 17% -> 20% of each run, Pallas kernels for 0% -> 0%
where the time goes in v1:
time: 103 us; the launch traced here: 102 us
  waiting for transfers between devices  45 us (44%)
  starting transfers between devices  22.8 us (22%)
  local copies, waits for them, and re-layouts  22.2 us (22%)
  blocking collectives  4.81 us (5%)
  matrix products  4.56 us (4%)
  other arithmetic  2.53 us (2%)
    all_to_all x1, waiting for transfers between devices, per_device(): lax.all_to_all(value_up, ('wt', 'sub'), split_axis=0, concat_axis=1, tile...  30 us
    all_to_all x2, waiting for transfers between devices, serve(): lax.all_to_all(latent_cache[safe], 'ctx', split_axis=0, concat_axis=0, ti...  14 us
    ppermute x6, starting transfers between devices, manage_the_steps_all(): ppermute(all_values, mesh_ax, [(dev_i, dev_i ^ tick) for dev_i in range(c...  10.2 us
    all_to_all x2, starting transfers between devices, serve(): lax.all_to_all(latent_cache[safe], 'ctx', split_axis=0, concat_axis=0, ti...  7.69 us
    dynamic_update_slice x8, local copies, waits for them, and re-layouts, manage_the_steps_all(): lax.dynamic_update_slice_in_dim(everything, all_values, (later ^ tick) *...  5.69 us
    all_to_all x1, starting transfers between devices, per_device(): lax.all_to_all(value_up, ('wt', 'sub'), split_axis=0, concat_axis=1, tile...  4.86 us
    all_gather x2, blocking collectives, fetch(): fetched = lax.all_gather(fetched, 'sub', axis=2, tiled=True)  4.81 us
    slice x1, local copies, waits for them, and re-layouts, per_device(): queries[index]  3.08 us
  transfers between devices with their start and end apart: 9, of which 4 were waited for; matrix products, arithmetic and copies ran while one was open for 20% of the time, Pallas kernels for 0%

profile of v1, /device:TPU:0, one launch (start us, length us, event | category | flops | bytes accessed | tf_op | source)
XLA Modules:
  0.0 102.1 jit_solution(18001123323923653473)
XLA Ops:
  0.0 0.8 fusion.13
  0.8 0.7 constant_dynamic-slice_fusion
  1.5 5.1 %collective-permute-start.5 = (s32[1,1]{0,1:T(1,128)}, s32[1,1]{0,1:T(1,128)}, u32[]{:S(2)}, u32[]{:S(2)}) collective-permute-start(s32[1,1]{0,1:T(1,128)} %bitcast.14), channel_id=1, source_target_pairs={{0,12},{4,8},{8,4},{12,0},{1,13},{5,9},{9,5},{13,1},{2,14},{6,10},... | collective-permute-start | bytes 20 | tf_op jit(solution)/shard_map/ppermute | solution.py:60
  7.8 3.8 %collective-permute-start.2 = (s32[1,1]{0,1:T(1,128)}, s32[1,1]{0,1:T(1,128)}, u32[]{:S(2)}, u32[]{:S(2)}) collective-permute-start(s32[1,1]{0,1:T(1,128)} %bitcast.4), channel_id=1, source_target_pairs={{0,12},{4,8},{8,4},{12,0},{1,13},{5,9},{9,5},{13,1},{2,14},{6,10},... | collective-permute-start | bytes 20 | tf_op jit(solution)/shard_map/ppermute | solution.py:60
  11.6 0.7 dynamic_update_slice.28
  12.3 0.7 dynamic_update_slice.24
  13.0 0.7 collective-permute-start
  13.8 0.7 dynamic_update_slice.29
  15.8 1.0 collective-permute-done
  16.8 0.8 dynamic_update_slice.25
  18.3 0.7 dynamic_update_slice.27
  19.1 1.3 %gather_fusion.2 = bf16[4,64,576]{2,1,0:T(8,128)(2,1)} fusion(bf16[16,64,576]{2,1,0:T(8,128)(2,1)S(1)} %copy-done, s32[1024]{0:T(1024)S(1)} %pad_clamp_fusion.1), kind=kCustom, calls=%fused_computation.2 | custom fusion | bytes 589840 | tf_op jit(solution)/shard_map/gather | solution.py:40
  20.4 4.2 %all-to-all-start.1 = ((bf16[4,1,64,576]{3,2,1,0:T(8,128)(2,1)}), bf16[4,1,64,576]{3,2,1,0:T(8,128)(2,1)S(1)}, u32[]{:S(2)}, u32[]{:S(2)}) async-start(bf16[4,1,64,576]{3,2,1,0:T(8,128)(2,1)} %bitcast.16), calls=%async_computation.1 | async-start | bytes 655360 | tf_op jit(solution)/shard_map/all_to_all | solution.py:40
  24.6 1.3 %gather_fusion = bf16[4,64,576]{2,1,0:T(8,128)(2,1)} fusion(bf16[16,64,576]{2,1,0:T(8,128)(2,1)S(1)} %copy-done, s32[1024]{0:T(1024)S(1)} %pad_clamp_fusion.3), kind=kCustom, calls=%fused_computation | custom fusion | bytes 589840 | tf_op jit(solution)/shard_map/gather | solution.py:40
  25.9 7.1 %all-to-all-done.1 = bf16[4,1,64,576]{3,2,1,0:T(8,128)(2,1)S(1)} async-done(((bf16[4,1,64,576]{3,2,1,0:T(8,128)(2,1)}), bf16[4,1,64,576]{3,2,1,0:T(8,128)(2,1)S(1)}, u32[]{:S(2)}, u32[]{:S(2)}) %all-to-all-start.1) | async-done | bytes 294944 | tf_op jit(solution)/shard_map/all_to_all | solution.py:40
  33.0 3.5 %all-to-all-start = ((bf16[4,1,64,576]{3,2,1,0:T(8,128)(2,1)}), bf16[4,1,64,576]{3,2,1,0:T(8,128)(2,1)S(1)}, u32[]{:S(2)}, u32[]{:S(2)}) async-start(bf16[4,1,64,576]{3,2,1,0:T(8,128)(2,1)} %bitcast.6), calls=%async_computation | async-start | bytes 655360 | tf_op jit(solution)/shard_map/all_to_all | solution.py:40
  36.9 6.9 %all-to-all-done = bf16[4,1,64,576]{3,2,1,0:T(8,128)(2,1)S(1)} async-done(((bf16[4,1,64,576]{3,2,1,0:T(8,128)(2,1)}), bf16[4,1,64,576]{3,2,1,0:T(8,128)(2,1)S(1)}, u32[]{:S(2)}, u32[]{:S(2)}) %all-to-all-start) | async-done | bytes 294944 | tf_op jit(solution)/shard_map/all_to_all | solution.py:40
  43.7 0.7 copy-done.2
  44.5 4.9 %all-to-all-start.2 = ((bf16[128,128,128]{2,1,0:T(8,128)(2,1)}), bf16[128,128,128]{2,1,0:T(8,128)(2,1)}, u32[]{:S(2)}, u32[]{:S(2)}) async-start(bf16[128,128,128]{2,1,0:T(8,128)(2,1)} %param.7), calls=%async_computation.2 | async-start | bytes 8388608 | tf_op jit(solution)/shard_map/all_to_all | solution.py:77
  49.4 1.0 sort.31
  50.4 1.0 sort.32
  51.4 3.1 %fusion.12 = (bf16[1,32,32,576]{3,2,1,0:T(8,128)(2,1)S(1)}, bf16[1,32,32,576]{3,2,1,0:T(8,128)(2,1)}) fusion(bf16[2,32,32,576]{3,2,1,0:T(8,128)(2,1)} %param.4), kind=kLoop, calls=%fused_computation.42 | loop fusion | bytes 4718592 | tf_op jit(solution)/shard_map/slice | solution.py:75
  54.5 2.3 %all-gather = bf16[4,2,64,576]{3,2,1,0:T(8,128)(2,1)S(1)} all-gather(bf16[4,1,64,576]{3,2,1,0:T(8,128)(2,1)S(1)} %copy-done.3), channel_id=2, replica_groups=mesh['groups'=2,'ctx'=4,'wt'=2,'sub'=2] {'sub'}, dimensions={1}, use_global_device_ids=true | all-gather | bytes 884736 | tf_op jit(solution)/shard_map/all_gather | solution.py:70
  56.8 1.3 %gather_fusion.1 = bf16[4,64,576]{2,1,0:T(8,128)(2,1)} fusion(bf16[8,64,576]{2,1,0:T(8,128)(2,1)S(1)} %bitcast.42, s32[1024]{0:T(1024)S(1)} %pad_clamp_fusion.2), kind=kCustom, calls=%fused_computation.1 | custom fusion | bytes 589840 | tf_op jit(solution)/shard_map/gather | solution.py:19
  58.1 2.5 %all-gather.1 = bf16[4,2,64,576]{3,2,1,0:T(8,128)(2,1)S(1)} all-gather(bf16[4,1,64,576]{3,2,1,0:T(8,128)(2,1)} %copy-done.1), channel_id=3, replica_groups=mesh['groups'=2,'ctx'=4,'wt'=2,'sub'=2] {'sub'}, dimensions={1}, use_global_device_ids=true | all-gather | bytes 884736 | tf_op jit(solution)/shard_map/all_gather | solution.py:70
  60.6 1.3 %gather_fusion.3 = bf16[4,64,576]{2,1,0:T(8,128)(2,1)} fusion(bf16[8,64,576]{2,1,0:T(8,128)(2,1)S(1)} %bitcast.43, s32[1024]{0:T(1024)S(1)} %pad_clamp_fusion), kind=kCustom, calls=%fused_computation.3 | custom fusion | bytes 589840 | tf_op jit(solution)/shard_map/gather | solution.py:19
  61.9 2.1 %fusion.14 = (f32[1024]{0:T(1024)S(1)}, f32[256,1024]{1,0:T(8,128)S(1)}) fusion(bf16[256,576]{1,0:T(8,128)(2,1)} %bitcast.46, bf16[1024,576]{1,0:T(8,128)(2,1)} %bitcast.40), kind=kOutput, calls=%fused_computation.44 | convolution fusion | flops 302513152 | bytes 2527232 | tf_op jit(solution)/shard_map/rd,kd->rk/dot_general | solution.py:21
  66.3 1.2 %copy.12 = bf16[2,32,32,512]{3,1,0,2:T(8,128)(2,1)S(1)} copy(bf16[2,32,32,512]{3,2,1,0:T(8,128)(2,1)S(1)} %pad_maximum_fusion) | data formatting | bytes 4194304 | tf_op jit(solution)/shard_map/stack | solution.py:76
  67.5 30.0 %all-to-all-done.2 = bf16[128,128,128]{2,1,0:T(8,128)(2,1)} async-done(((bf16[128,128,128]{2,1,0:T(8,128)(2,1)}), bf16[128,128,128]{2,1,0:T(8,128)(2,1)}, u32[]{:S(2)}, u32[]{:S(2)}) %all-to-all-start.2) | async-done | bytes 4194336 | tf_op jit(solution)/shard_map/all_to_all | solution.py:77
  97.6 2.5 %copy.13 = bf16[4,32,128,128]{3,2,0,1:T(8,128)(2,1)S(1)} copy(bf16[4,32,128,128]{3,2,1,0:T(8,128)(2,1)} %bitcast.22) | data formatting | bytes 8388608 | tf_op jit(solution)/shard_map/all_to_all | solution.py:77
  100.1 0.9 convolution_convert_fusion
  100.9 1.1 %copy.14 = bf16[2,32,32,128]{3,2,1,0:T(8,128)(2,1)} copy(bf16[2,32,32,128]{3,1,0,2:T(8,128)(2,1)S(1)} %bitcast.41) | data formatting | bytes 1048576 | tf_op jit(solution)/shard_map/reshape | solution.py:79
  (49 shorter events, 6.0 us)
Async XLA Ops:
  0.0 19.1 %copy-start = (bf16[16,64,576]{2,1,0:T(8,128)(2,1)S(1)}, bf16[16,64,576]{2,1,0:T(8,128)(2,1)}, u32[]{:S(2)}) copy-start(bf16[16,64,576]{2,1,0:T(8,128)(2,1)} %param.6) | copy-start | bytes 3538948
  0.0 36.5 %copy-start.6 = (s32[2,4,2]{1,2,0:T(2,128)S(1)}, s32[2,4,2]{1,2,0:T(2,128)}, u32[]{:S(2)}) copy-start(s32[2,4,2]{1,2,0:T(2,128)} %param.5) | copy-start | bytes 196
  1.5 13.7 %collective-permute-start.5 = (s32[1,1]{0,1:T(1,128)}, s32[1,1]{0,1:T(1,128)}, u32[]{:S(2)}, u32[]{:S(2)}) collective-permute-start(s32[1,1]{0,1:T(1,128)} %bitcast.14), channel_id=1, source_target_pairs={{0,12},{4,8},{8,4},{12,0},{1,13},{5,9},{9,5},{13,1},{2,14},{6,10},... | collective-permute-start | bytes 20 | tf_op jit(solution)/shard_map/ppermute | solution.py:60
  6.6 7.9 %collective-permute-start.4 = (s32[1,1]{0,1:T(1,128)}, s32[1,1]{0,1:T(1,128)}, u32[]{:S(2)}, u32[]{:S(2)}) collective-permute-start(s32[1,1]{0,1:T(1,128)} %bitcast.13), channel_id=1, source_target_pairs={{0,8},{4,12},{8,0},{12,4},{1,9},{5,13},{9,1},{13,5},{2,10},{6,14},... | collective-permute-start | bytes 20 | tf_op jit(solution)/shard_map/ppermute | solution.py:60
  6.6 6.4 %collective-permute-start.3 = (s32[1,1]{0,1:T(1,128)}, s32[1,1]{0,1:T(1,128)}, u32[]{:S(2)}, u32[]{:S(2)}) collective-permute-start(s32[1,1]{0,1:T(1,128)} %bitcast.12), channel_id=1, source_target_pairs={{0,4},{4,0},{8,12},{12,8},{1,5},{5,1},{9,13},{13,9},{2,6},{6,2},{1... | collective-permute-start | bytes 20 | tf_op jit(solution)/shard_map/ppermute | solution.py:60
  7.8 10.5 %collective-permute-start.2 = (s32[1,1]{0,1:T(1,128)}, s32[1,1]{0,1:T(1,128)}, u32[]{:S(2)}, u32[]{:S(2)}) collective-permute-start(s32[1,1]{0,1:T(1,128)} %bitcast.4), channel_id=1, source_target_pairs={{0,12},{4,8},{8,4},{12,0},{1,13},{5,9},{9,5},{13,1},{2,14},{6,10},... | collective-permute-start | bytes 20 | tf_op jit(solution)/shard_map/ppermute | solution.py:60
  11.6 6.0 %collective-permute-start.1 = (s32[1,1]{0,1:T(1,128)}, s32[1,1]{0,1:T(1,128)}, u32[]{:S(2)}, u32[]{:S(2)}) collective-permute-start(s32[1,1]{0,1:T(1,128)} %bitcast.3), channel_id=1, source_target_pairs={{0,8},{4,12},{8,0},{12,4},{1,9},{5,13},{9,1},{13,5},{2,10},{6,14},... | collective-permute-start | bytes 20 | tf_op jit(solution)/shard_map/ppermute | solution.py:60
  13.0 3.8 %collective-permute-start = (s32[1,1]{0,1:T(1,128)}, s32[1,1]{0,1:T(1,128)}, u32[]{:S(2)}, u32[]{:S(2)}) collective-permute-start(s32[1,1]{0,1:T(1,128)} %bitcast.2), channel_id=1, source_target_pairs={{0,4},{4,0},{8,12},{12,8},{1,5},{5,1},{9,13},{13,9},{2,6},{6,2},{1... | collective-permute-start | bytes 20 | tf_op jit(solution)/shard_map/ppermute | solution.py:60
  20.4 12.6 %all-to-all-start.1 = ((bf16[4,1,64,576]{3,2,1,0:T(8,128)(2,1)}), bf16[4,1,64,576]{3,2,1,0:T(8,128)(2,1)S(1)}, u32[]{:S(2)}, u32[]{:S(2)}) async-start(bf16[4,1,64,576]{3,2,1,0:T(8,128)(2,1)} %bitcast.16), calls=%async_computation.1 | async-start | bytes 655360 | tf_op jit(solution)/shard_map/all_to_all | solution.py:40
  33.0 10.7 %copy-start.1 = (bf16[4,1,64,576]{3,2,1,0:T(8,128)(2,1)}, bf16[4,1,64,576]{3,2,1,0:T(8,128)(2,1)S(1)}, u32[]{:S(2)}) copy-start(bf16[4,1,64,576]{3,2,1,0:T(8,128)(2,1)S(1)} %all-to-all-done.1) | copy-start | bytes 884740
  33.0 10.7 %all-to-all-start = ((bf16[4,1,64,576]{3,2,1,0:T(8,128)(2,1)}), bf16[4,1,64,576]{3,2,1,0:T(8,128)(2,1)S(1)}, u32[]{:S(2)}, u32[]{:S(2)}) async-start(bf16[4,1,64,576]{3,2,1,0:T(8,128)(2,1)} %bitcast.6), calls=%async_computation | async-start | bytes 655360 | tf_op jit(solution)/shard_map/all_to_all | solution.py:40
  43.7 0.8 copy-start.2
  44.5 53.1 %all-to-all-start.2 = ((bf16[128,128,128]{2,1,0:T(8,128)(2,1)}), bf16[128,128,128]{2,1,0:T(8,128)(2,1)}, u32[]{:S(2)}, u32[]{:S(2)}) async-start(bf16[128,128,128]{2,1,0:T(8,128)(2,1)} %param.7), calls=%async_computation.2 | async-start | bytes 8388608 | tf_op jit(solution)/shard_map/all_to_all | solution.py:77
  51.4 3.1 %copy-start.3 = (bf16[4,1,64,576]{3,2,1,0:T(8,128)(2,1)S(1)}, bf16[4,1,64,576]{3,2,1,0:T(8,128)(2,1)}, u32[]{:S(2)}) copy-start(bf16[4,1,64,576]{3,2,1,0:T(8,128)(2,1)} %copy-done.2) | copy-start | bytes 884740
  61.9 2.3 %copy-start.4 = (bf16[4,64,576]{2,1,0:T(8,128)(2,1)S(1)}, bf16[4,64,576]{2,1,0:T(8,128)(2,1)}, u32[]{:S(2)}) copy-start(bf16[4,64,576]{2,1,0:T(8,128)(2,1)} %gather_fusion.1) | copy-start | bytes 884740
  64.2 1.0 copy-start.5
